TPU v7x, 256 devices: a whole 4x4x8 slice. The times are simulated.
256 devices in a mesh: blk: 16 (over z, core), red: 16 (over x, y).
Axes of the slice: x: 4, y: 4, z: 8, core: 2. Of those that a mesh axis runs over, the one named last changes fastest.
Arguments:
- amplitudes: bfloat16 [8, 192, 128, 128], P(None, 'blk', 'red'), may hold values from -6 to 6
- ladder_ints: bfloat16 [16384, 16384], P('red', 'blk'), may hold values from -0.046875 to 0.046875
- cycle_ints: bfloat16 [24576, 24576], P('blk', 'red'), may hold values from -0.0390625 to 0.0390625
- occ_energy: float32 [192], replicated, may hold values from -2 to -0.3
- vir_energy: float32 [128], replicated, may hold values from 0.2 to 3
- slab_index: int32 [8], replicated, may hold values from 0 to 191
Outputs:
- update: float32 [8, 192, 128, 128], P(None, 'red', 'blk')
All inputs are finite; a program needn't handle non-finite values.
Results may differ from a plain program's by a relative error of at most 0.0003.
Values may be sent and summed in bfloat16 or wider, within the bound.
A program may use at most 64 MiB of HBM per device.

v0:
```python
import jax
import jax.numpy as jnp
from jax import lax
from jax.sharding import PartitionSpec as P


def shards(amplitudes, ladder_ints, cycle_ints, occ_energy, vir_energy, slab_index):
    slab_rows, occ_local, vir_local, virt_width = amplitudes.shape
    occ_all = occ_local * lax.axis_size("blk")
    occ_red = occ_all // lax.axis_size("red")
    shard_piece = lax.all_gather(amplitudes, "blk", axis=1, tiled=True)
    row_count = shard_piece.shape[1]
    flattened = shard_piece.reshape(slab_rows * row_count, vir_local * virt_width)
    product = jnp.dot(flattened, ladder_ints, preferred_element_type=jnp.float32)
    ladder = product.reshape(slab_rows, row_count, ladder_ints.shape[1])
    ladder_own = lax.psum_scatter(ladder, "red", scatter_dimension=1, tiled=True)
    ladder_own = ladder_own.reshape(slab_rows, occ_red, -1, virt_width)
    shard_piece = lax.all_gather(amplitudes, "red", axis=2, tiled=True)
    vir_count = shard_piece.shape[2]
    operand = jnp.transpose(shard_piece, (0, 2, 1, 3)).reshape(
        slab_rows * vir_count, occ_local * virt_width
    )
    product = jnp.dot(operand, cycle_ints, preferred_element_type=jnp.float32)
    cycle_term = product.reshape(slab_rows, vir_count, cycle_ints.shape[1])
    cycle_own = lax.psum_scatter(cycle_term, "blk", scatter_dimension=1, tiled=True)
    vir_block = cycle_own.shape[1]
    cycle_own = jnp.transpose(
        cycle_own.reshape(slab_rows, vir_block, occ_red, virt_width), (0, 2, 1, 3)
    )
    orbital_ids = jnp.arange(occ_energy.shape[0], dtype=jnp.int32)
    chosen = slab_index[:, None] == orbital_ids[None, :]
    slab_energy = jnp.sum(jnp.where(chosen, occ_energy[None, :], jnp.float32(0.0)), axis=1)
    pair_energy = lax.dynamic_slice_in_dim(occ_energy, lax.axis_index("red") * occ_red, occ_red)
    first_virtual = lax.dynamic_slice_in_dim(
        vir_energy, lax.axis_index("blk") * vir_block, vir_block
    )
    denominator = (
        first_virtual[None, None, :, None]
        + vir_energy[None, None, None, :]
        - slab_energy[:, None, None, None]
        - pair_energy[None, :, None, None]
    )
    return (ladder_own + cycle_own) / denominator


def solution(mesh):
    placed = (P(None, "blk", "red", None), P("red", "blk"), P("blk", "red"), P(), P(), P())
    return jax.shard_map(
        shards, mesh=mesh, in_specs=placed, out_specs=P(None, "red", "blk", None), check_vma=False
    )
```

profile of v0, /device:TPU:1, one launch (start us, length us, event | category | flops | bytes accessed | tf_op | source)
XLA Modules:
  0.0 272.5 jit_solution(8363558085387435878)
XLA Ops:
  6.5 0.0 copy-start
  6.5 0.0 all-gather.5.cloned.1.call-start
  6.5 1.8 copy.20
  8.4 0.0 all-gather.5.cloned.1.call-update
  8.4 0.0 all-gather.3.cloned.1.call-start
  8.4 0.7 all-gather.3.cloned.1.call-update
  9.1 0.0 reduce-scatter.5.cloned.1.call-start
  9.2 57.1 %all-gather.5.cloned.1.call-done = bf16[8,12,128,128]{3,0,1,2:T(8,128)(2,1)} async-done(((bf16[8,12,8,128]{3,0,1,2:T(8,128)(2,1)}), bf16[8,12,128,128]{3,0,1,2:T(8,128)(2,1)}) %all-gather.5.cloned.1.call-update) | async-done | bytes 3145744 | tf_op jit(solution)/shard_map/all_gather | solution.py:18
  66.3 5.0 %copy.21 = bf16[8,12,128,128]{2,3,1,0:T(8,128)(2,1)} copy(bf16[8,12,128,128]{3,0,1,2:T(8,128)(2,1)} %all-gather.5.cloned.1.call-done) | data formatting | bytes 6291456 | tf_op jit(solution)/shard_map/all_gather | solution.py:18
  71.3 9.8 %fusion = f32[8,128,1536]{2,1,0:T(8,128)} fusion(bf16[8,128,1536]{1,2,0:T(8,128)(2,1)} %bitcast.26, bf16[1536,1536]{1,0:T(8,128)(2,1)} %param.8), kind=kOutput, calls=%fused_computation | convolution fusion | flops 4831838208 | bytes 14155776 | tf_op jit(solution)/shard_map/dot_general | solution.py:23
  81.1 0.0 reduce-scatter.5.cloned.1.call-update
  81.1 0.0 reduce-scatter.3.cloned.1.call-start
  81.2 27.7 %all-gather.3.cloned.1.call-done = bf16[8,192,8,128]{3,2,1,0:T(8,128)(2,1)} async-done(((bf16[8,12,8,128]{3,2,1,0:T(8,128)(2,1)}), bf16[8,192,8,128]{3,2,1,0:T(8,128)(2,1)}) %all-gather.3.cloned.1.call-update) | async-done | bytes 3145744 | tf_op jit(solution)/shard_map/all_gather | solution.py:11
  108.9 5.8 %dot_general.10 = bf16[8,192,1024]{2,1,0:T(8,128)(2,1)} reshape(bf16[8,192,8,128]{3,2,1,0:T(8,128)(2,1)} %all-gather.3.cloned.1.call-done) | data formatting | bytes 6291456 | tf_op jit(solution)/shard_map/dot_general | solution.py:14
  114.7 0.0 copy-done
  114.7 7.9 %fusion.2 = f32[8,192,1024]{2,0,1:T(8,128)} fusion(bf16[8,192,1024]{2,1,0:T(8,128)(2,1)} %dot_general.10, bf16[1024,1024]{1,0:T(8,128)(2,1)S(1)} %copy-done), kind=kOutput, calls=%fused_computation.2 | convolution fusion | flops 3221225472 | bytes 11534336 | tf_op jit(solution)/shard_map/dot_general | solution.py:14
  122.6 0.0 copy-start.2
  122.6 0.0 copy-start.1
  122.6 0.0 copy-start.3
  122.6 0.0 reduce-scatter.3.cloned.1.call-update
  122.7 0.6 copy-done.2
  123.3 0.1 dynamic_slice.6
  123.4 0.0 copy-done.1
  123.4 0.1 dynamic_slice.7
  123.4 0.0 copy-done.3
  123.4 0.2 select_reduce_fusion
  123.6 0.1 broadcast_add_fusion
  123.7 0.1 broadcast_subtract_fusion
  123.8 49.4 %reduce-scatter.5.cloned.1.call-done = f32[8,8,1536]{2,1,0:T(8,128)} async-done(((f32[8,128,1536]{2,1,0:T(8,128)}), f32[8,8,1536]{2,1,0:T(8,128)}) %reduce-scatter.5.cloned.1.call-update) | async-done | bytes 393232 | tf_op jit(solution)/shard_map/reduce_scatter | solution.py:25
  173.2 90.8 %reduce-scatter.3.cloned.1.call-done = f32[8,12,1024]{2,0,1:T(8,128)} async-done(((f32[8,192,1024]{2,0,1:T(8,128)}), f32[8,12,1024]{2,0,1:T(8,128)}) %reduce-scatter.3.cloned.1.call-update) | async-done | bytes 393232 | tf_op jit(solution)/shard_map/reduce_scatter | solution.py:16
  264.0 1.3 fusion.5
  265.2 0.8 copy.24
Async XLA Ops:
  6.5 108.1 %copy-start = (bf16[1024,1024]{1,0:T(8,128)(2,1)S(1)}, bf16[1024,1024]{1,0:T(8,128)(2,1)}, u32[]{:S(2)}) copy-start(bf16[1024,1024]{1,0:T(8,128)(2,1)} %param.7) | copy-start | bytes 6291460
  6.5 59.8 %all-gather.5.cloned.1.call-start = ((), (), s32[]{:S(2)}) async-start(), calls=%async_computation.4 | async-start | bytes 3342336 | tf_op jit(solution)/shard_map/all_gather | solution.py:18
  8.4 100.5 %all-gather.3.cloned.1.call-start = ((), (), s32[]{:S(2)}) async-start(), calls=%async_computation.2 | async-start | bytes 3342336 | tf_op jit(solution)/shard_map/all_gather | solution.py:11
  9.1 164.1 %reduce-scatter.5.cloned.1.call-start = ((), (), s32[]{:S(2)}) async-start(), calls=%async_computation.5 | async-start | bytes 6684672 | tf_op jit(solution)/shard_map/reduce_scatter | solution.py:25
  81.1 182.9 %reduce-scatter.3.cloned.1.call-start = ((), (), s32[]{:S(2)}) async-start(), calls=%async_computation.3 | async-start | bytes 6684672 | tf_op jit(solution)/shard_map/reduce_scatter | solution.py:16
  122.6 0.7 copy-start.2
  122.6 0.7 copy-start.1
  122.6 0.8 copy-start.3
Sparse Core Ops, SparseCore 0:
  9.8 56.4 all-gather.4
  68.2 40.6 all-gather.2
  111.5 61.7 reduce-scatter.4
  176.8 87.1 reduce-scatter.2
where the time goes:
time: 273 us
  waiting for transfers between devices  226 us (83%)
  matrix products  17.7 us (6%)
  local copies, waits for them, and re-layouts  14.1 us (5%)
  between operations  13.1 us (5%)
    reduce_scatter x1, waiting for transfers between devices, shards(): lax.psum_scatter(ladder, 'red', scatter_dimension=1, tiled=True)  90.8 us
    all_gather x1, waiting for transfers between devices, shards(): shard_piece = lax.all_gather(amplitudes, 'red', axis=2, tiled=True)  57.1 us
    reduce_scatter x1, waiting for transfers between devices, shards(): lax.psum_scatter(cycle_term, 'blk', scatter_dimension=1, tiled=True)  49.4 us
    all_gather x1, waiting for transfers between devices, shards(): shard_piece = lax.all_gather(amplitudes, 'blk', axis=1, tiled=True)  27.7 us
    dot_general x1, matrix products, shards(): product = jnp.dot(operand, cycle_ints, preferred_element_type=jnp.float32)  9.79 us
    dot_general x1, matrix products, shards(): jnp.dot(flattened, ladder_ints, preferred_element_type=jnp.float32)  7.95 us
    dot_general x1, local copies, waits for them, and re-layouts, shards(): jnp.dot(flattened, ladder_ints, preferred_element_type=jnp.float32)  5.78 us
  transfers between devices with their start and end apart: 4, of which 4 were waited for; matrix products, arithmetic and copies ran while one was open for 11% of the time, Pallas kernels for 0%

commit v1 on v0

--- a/solution.py
+++ b/solution.py
@@ -8,7 +8,15 @@
     slab_rows, occ_local, vir_local, virt_width = amplitudes.shape
     occ_all = occ_local * lax.axis_size("blk")
     occ_red = occ_all // lax.axis_size("red")
-    shard_piece = lax.all_gather(amplitudes, "blk", axis=1, tiled=True)
+    shard_piece = jnp.concatenate(
+        lax.all_to_all(
+            jnp.stack(tuple((amplitudes for _ in range(lax.psum(1, axis_name="blk"))))),
+            axis_name="blk",
+            split_axis=0,
+            concat_axis=0,
+        ),
+        axis=1,
+    )
     row_count = shard_piece.shape[1]
     flattened = shard_piece.reshape(slab_rows * row_count, vir_local * virt_width)
     product = jnp.dot(flattened, ladder_ints, preferred_element_type=jnp.float32)

time: 273 us -> 301 us (1.10)
  blocking collectives: 0 us -> 97.8 us
  waiting for transfers between devices: 226 us -> 152 us
  local copies, waits for them, and re-layouts: 14.1 us -> 18.2 us
    all_to_all x0 -> x1, blocking collectives: none -> 97.8 us  [shards(): lax.all_to_all(jnp.stack(tuple((amplitudes for _ in range(lax.psum(1, axi...]
    reduce_scatter x1, waiting for transfers between devices: 49.4 us -> 4.54 us  [shards(): lax.psum_scatter(cycle_term, 'blk', scatter_dimension=1, tiled=True)]
    all_gather x1 -> x0, waiting for transfers between devices: 27.7 us -> none  [shards(): shard_piece = lax.all_gather(amplitudes, 'blk', axis=1, tiled=True)]
    dot_general x1 -> x2, local copies, waits for them, and re-layouts: 5.78 us -> 8.39 us  [shards(): jnp.dot(flattened, ladder_ints, preferred_element_type=jnp.float32)]
  transfers between devices with their start and end apart: 4 -> 3, of which waited for: 4 -> 3; matrix products, arithmetic and copies ran while one was open for 11% -> 6% of each run, Pallas kernels for 0% -> 0%
where the time goes in v1:
time: 301 us; the launch traced here: 300 us
  waiting for transfers between devices  152 us (50%)
  blocking collectives  97.8 us (32%)
  local copies, waits for them, and re-layouts  18.2 us (6%)
  matrix products  17 us (6%)
  between operations  13.1 us (4%)
    all_to_all x1, blocking collectives, shards(): lax.all_to_all(jnp.stack(tuple((amplitudes for _ in range(lax.psum(1, axi...  97.8 us
    reduce_scatter x1, waiting for transfers between devices, shards(): lax.psum_scatter(ladder, 'red', scatter_dimension=1, tiled=True)  89.8 us
    all_gather x1, waiting for transfers between devices, shards(): shard_piece = lax.all_gather(amplitudes, 'red', axis=2, tiled=True)  57.9 us
    dot_general x1, matrix products, shards(): product = jnp.dot(operand, cycle_ints, preferred_element_type=jnp.float32)  9.79 us
    dot_general x2, local copies, waits for them, and re-layouts, shards(): jnp.dot(flattened, ladder_ints, preferred_element_type=jnp.float32)  8.39 us
    dot_general x1, matrix products, shards(): jnp.dot(flattened, ladder_ints, preferred_element_type=jnp.float32)  7.26 us
  transfers between devices with their start and end apart: 3, of which 3 were waited for; matrix products, arithmetic and copies ran while one was open for 6% of the time, Pallas kernels for 0%

profile of v1, /device:TPU:1, one launch (start us, length us, event | category | flops | bytes accessed | tf_op | source)
XLA Modules:
  0.0 300.1 jit_solution(4318035991805836494)
XLA Ops:
  6.5 0.0 copy-start
  6.5 0.0 all-gather.2.cloned.1.call-start
  6.5 1.8 copy.22
  8.4 0.0 all-gather.2.cloned.1.call-update
  8.4 0.0 reduce-scatter.5.cloned.1.call-start
  8.4 57.9 %all-gather.2.cloned.1.call-done = bf16[8,12,128,128]{3,0,1,2:T(8,128)(2,1)} async-done(((bf16[8,12,8,128]{3,0,1,2:T(8,128)(2,1)}), bf16[8,12,128,128]{3,0,1,2:T(8,128)(2,1)}) %all-gather.2.cloned.1.call-update) | async-done | bytes 3145744 | tf_op jit(solution)/shard_map/all_gather | solution.py:26
  66.3 4.9 %copy.23 = bf16[8,12,128,128]{2,3,1,0:T(8,128)(2,1)} copy(bf16[8,12,128,128]{3,0,1,2:T(8,128)(2,1)} %all-gather.2.cloned.1.call-done) | data formatting | bytes 6291456 | tf_op jit(solution)/shard_map/all_gather | solution.py:26
  71.3 9.8 %fusion = f32[8,128,1536]{2,1,0:T(8,128)} fusion(bf16[8,128,1536]{1,2,0:T(8,128)(2,1)} %bitcast.31, bf16[1536,1536]{1,0:T(8,128)(2,1)} %param.8), kind=kOutput, calls=%fused_computation | convolution fusion | flops 4831838208 | bytes 14155776 | tf_op jit(solution)/shard_map/dot_general | solution.py:31
  81.0 0.0 copy-start.1
  81.0 0.0 reduce-scatter.5.cloned.1.call-update
  81.1 0.0 reduce-scatter.3.cloned.1.call-start
  81.1 0.9 copy-done.1
  82.0 0.6 stack.2
  82.6 97.8 %all_to_all.5 = bf16[16,8,12,8,128]{4,3,2,1,0:T(8,128)(2,1)S(1)} all-to-all(bf16[16,8,12,8,128]{4,3,2,1,0:T(8,128)(2,1)S(1)} %stack.2), channel_id=1, replica_groups=mesh['blk'=16,'red'=16] {'blk'}, dimensions={0} | all-to-all | bytes 6291456 | tf_op jit(solution)/shard_map/all_to_all | solution.py:12
  180.4 2.6 copy.30
  182.9 5.8 %reshape.65 = bf16[8,192,1024]{2,0,1:T(8,128)(2,1)} reshape(bf16[8,16,12,8,128]{4,3,0,2,1:T(8,128)(2,1)} %copy.30) | data formatting | bytes 6291456 | tf_op jit(solution)/shard_map/dot_general | solution.py:22
  188.8 0.0 copy-done
  188.8 7.3 %fusion.2 = f32[8,192,1024]{2,0,1:T(8,128)} fusion(bf16[8,192,1024]{2,0,1:T(8,128)(2,1)} %reshape.65, bf16[1024,1024]{1,0:T(8,128)(2,1)S(1)} %copy-done), kind=kOutput, calls=%fused_computation.2 | convolution fusion | flops 3221225472 | bytes 11534336 | tf_op jit(solution)/shard_map/dot_general | solution.py:22
  196.0 0.0 copy-start.2
  196.0 0.0 copy-start.3
  196.0 0.0 copy-start.4
  196.0 0.0 reduce-scatter.3.cloned.1.call-update
  196.1 0.6 copy-done.2
  196.7 0.1 dynamic_slice.7
  196.8 0.0 copy-done.3
  196.8 0.1 dynamic_slice.6
  196.8 0.0 copy-done.4
  196.8 0.2 select_reduce_fusion
  197.0 0.1 broadcast_add_fusion
  197.1 0.1 broadcast_subtract_fusion
  197.2 4.5 %reduce-scatter.5.cloned.1.call-done = f32[8,8,1536]{2,1,0:T(8,128)} async-done(((f32[8,128,1536]{2,1,0:T(8,128)}), f32[8,8,1536]{2,1,0:T(8,128)}) %reduce-scatter.5.cloned.1.call-update) | async-done | bytes 393232 | tf_op jit(solution)/shard_map/reduce_scatter | solution.py:33
  201.7 89.8 %reduce-scatter.3.cloned.1.call-done = f32[8,12,1024]{2,0,1:T(8,128)} async-done(((f32[8,192,1024]{2,0,1:T(8,128)}), f32[8,12,1024]{2,0,1:T(8,128)}) %reduce-scatter.3.cloned.1.call-update) | async-done | bytes 393232 | tf_op jit(solution)/shard_map/reduce_scatter | solution.py:24
  291.5 1.3 fusion.4
  292.8 0.8 copy.26
Async XLA Ops:
  6.5 182.2 %copy-start = (bf16[1024,1024]{1,0:T(8,128)(2,1)S(1)}, bf16[1024,1024]{1,0:T(8,128)(2,1)}, u32[]{:S(2)}) copy-start(bf16[1024,1024]{1,0:T(8,128)(2,1)} %param.7) | copy-start | bytes 6291460
  6.5 59.8 %all-gather.2.cloned.1.call-start = ((), (), s32[]{:S(2)}) async-start(), calls=%async_computation.4 | async-start | bytes 3342336 | tf_op jit(solution)/shard_map/all_gather | solution.py:26
  8.4 193.3 %reduce-scatter.5.cloned.1.call-start = ((), (), s32[]{:S(2)}) async-start(), calls=%async_computation.5 | async-start | bytes 6684672 | tf_op jit(solution)/shard_map/reduce_scatter | solution.py:33
  81.0 0.9 copy-start.1
  81.1 210.5 %reduce-scatter.3.cloned.1.call-start = ((), (), s32[]{:S(2)}) async-start(), calls=%async_computation.3 | async-start | bytes 6684672 | tf_op jit(solution)/shard_map/reduce_scatter | solution.py:24
  196.0 0.7 copy-start.2
  196.0 0.8 copy-start.3
  196.0 0.8 copy-start.4
Sparse Core Ops, SparseCore 0:
  9.8 56.4 all-gather.1
  81.2 120.4 reduce-scatter.4
  205.4 86.0 reduce-scatter.2
